TPU v7x, 256 devices: a whole 4x4x8 slice. The times are simulated.
256 devices in a mesh: grid: 8 (over y, core), wide: 32 (over z, x).
Axes of the slice: x: 4, y: 4, z: 8, core: 2. Of those that a mesh axis runs over, the one named last changes fastest.
Arguments:
- values: bfloat16 [3584, 64, 4096], P(('grid', 'wide')), may hold values from 0 to 1
- a_block: int32 [3584], P(('grid', 'wide')), may hold values from 0 to 63, as said below
- b_block: int32 [3584], P(('grid', 'wide')), may hold values from 0 to 15
- c_block: int32 [3584], P(('grid', 'wide')), may hold values from 0 to 63
- held: int32 [3584], P(('grid', 'wide')), may hold values from 0 to 1, as said below
- factor_a: bfloat16 [32768, 256], P(('grid', 'wide')), may hold values from -6 to 6
- factor_b: bfloat16 [32768, 256], P(('wide', 'grid')), may hold values from -2.390625 to 2.390625
- factor_c: bfloat16 [4096, 256], replicated, may hold values from -2.390625 to 2.390625
Outputs:
- next_a: float32 [32768, 256], P(('grid', 'wide'))
- next_b: float32 [32768, 256], P(('wide', 'grid'))
- held_loss: float32 [], replicated
Inputs may be any that keep to these rules, and one draw needn't show every extreme that they name: Among the blocks of one device, at most 1 have a_block values with the same a_block // 2; on some device some such value is shared by exactly 1 block. Every device holds 1 to 3 held-out blocks; some device holds exactly 3.
All inputs are finite; a program needn't handle non-finite values.
Results may differ from a plain program's by a relative error of at most 0.0011.
Values may be sent and summed in bfloat16 or wider, within the bound.
No kernel may reach another device: no remote copies, remote signals or barrier semaphores. Data moves between devices by JAX's collectives and lax.ppermute only.
A program may use at most 64 MiB of HBM per device.

v0:
```python
import jax
import jax.numpy as jnp
from jax import lax
from jax.sharding import PartitionSpec as P

step_size = 0.05


def block_terms(inputs):
    entries, a_rows, b_rows, c_rows, flag = inputs
    side = a_rows.shape[0]
    width = a_rows.shape[1]
    khatri = (
        b_rows.astype(jnp.float32)[:, None, :] * c_rows.astype(jnp.float32)[None, :, :]
    ).astype(jnp.bfloat16)
    khatri = khatri.reshape(side * side, width)
    model = lax.dot_general(
        a_rows, khatri, (((1,), (1,)), ((), ())), preferred_element_type=jnp.float32
    )
    entry_f = entries.astype(jnp.float32)
    resid = ((jax.nn.sigmoid(model) - entry_f) * (1.0 - flag)).astype(jnp.bfloat16)
    loss_part = jnp.sum(jax.nn.softplus(model) - entry_f * model) * flag
    grad_rows = jnp.dot(resid, khatri, preferred_element_type=jnp.float32)
    partial_sum = lax.dot_general(
        resid, a_rows, (((0,), (0,)), ((), ())), preferred_element_type=jnp.float32
    )
    grad_cols = jnp.sum(
        partial_sum.reshape(side, side, width) * c_rows.astype(jnp.float32)[None, :, :], axis=1
    )
    return (grad_rows, grad_cols, loss_part)


def per_device(values, a_block, b_block, c_block, held, factor_a, factor_b, factor_c):
    blocks = values.shape[0]
    side = values.shape[1]
    width = factor_a.shape[1]
    highest = lax.Precision.HIGHEST
    own_blocks = factor_a.shape[0] // side
    wide_count = lax.axis_size("wide")
    b_panel = lax.all_gather(factor_b, "grid", axis=0, tiled=True)
    b_rows = b_panel.reshape(-1, side, width)[b_block]
    c_rows = factor_c.reshape(-1, side, width)[c_block]
    a_panel = lax.all_gather(factor_a, "wide", axis=0, tiled=True)
    a_rows = a_panel.reshape(-1, side, width)[a_block]
    flags = held.astype(jnp.float32)
    grad_rows, grad_cols, loss_parts = lax.map(block_terms, (values, a_rows, b_rows, c_rows, flags))
    panel_blocks = own_blocks * wide_count
    matches = (a_block[:, None] == jnp.arange(panel_blocks)[None, :]).astype(jnp.float32)
    panel_grad = jnp.einsum("np,nk->pk", matches, grad_rows.reshape(blocks, -1), precision=highest)
    grad_a = lax.psum_scatter(
        panel_grad.reshape(panel_blocks * side, width), "wide", scatter_dimension=0, tiled=True
    )
    b_panel_blocks = b_panel.shape[0] // side
    b_matches = (b_block[:, None] == jnp.arange(b_panel_blocks)[None, :]).astype(jnp.float32)
    b_panel_grad = jnp.einsum(
        "np,nk->pk", b_matches, grad_cols.reshape(blocks, -1), precision=highest
    )
    grad_b = lax.psum_scatter(
        b_panel_grad.reshape(b_panel_blocks * side, width), "grid", scatter_dimension=0, tiled=True
    )
    loss_total, held_total = lax.psum((jnp.sum(loss_parts), jnp.sum(flags)), ("grid", "wide"))
    held_loss = loss_total / (held_total * (side * side * side))
    next_a = factor_a.astype(jnp.float32) - step_size * grad_a
    next_b = factor_b.astype(jnp.float32) - step_size * grad_b
    return (next_a, next_b, held_loss)


def solution(mesh):
    in_specs = (
        P(("grid", "wide"), None, None),
        P(("grid", "wide")),
        P(("grid", "wide")),
        P(("grid", "wide")),
        P(("grid", "wide")),
        P(("grid", "wide"), None),
        P(("wide", "grid"), None),
        P(),
    )
    out_specs = (P(("grid", "wide"), None), P(("wide", "grid"), None), P())
    return jax.shard_map(
        per_device, mesh=mesh, in_specs=in_specs, out_specs=out_specs, check_vma=False
    )
```

profile of v0, /device:TPU:8, one launch (start us, length us, event | category | flops | bytes accessed | tf_op | source)
XLA Modules:
  0.0 559.0 jit_solution(8834478500784365606)
XLA Ops:
  10.6 13.5 %all_gather.7 = bf16[1024,256]{1,0:T(8,128)(2,1)S(1)} all-gather(bf16[128,256]{1,0:T(8,128)(2,1)} %param.16), channel_id=1, replica_groups=mesh['grid'=8,'wide'=32] {'grid'}, dimensions={0}, use_global_device_ids=true | all-gather | bytes 589824 | tf_op jit(solution)/shard_map/all_gather | solution.py:40
  25.5 66.0 %all-gather.2.cloned.1.call-done = bf16[4096,256]{1,0:T(8,128)(2,1)} async-done(((bf16[128,256]{1,0:T(8,128)(2,1)}), bf16[4096,256]{1,0:T(8,128)(2,1)}) %all-gather.2.cloned.1.call-update) | async-done | bytes 2097168 | tf_op jit(solution)/shard_map/all_gather | solution.py:43
  91.5 2.9 gather_fusion
  94.4 195.9 %while.14 = (s32[]{:T(128)}, f32[14,64,256]{2,1,0:T(8,128)}, f32[14,64,256]{2,1,0:T(8,128)}, f32[14]{0:T(128)S(1)}, bf16[14,64,256]{2,1,0:T(8,128)(2,1)}, /*inde...) while((s32[]{:T(128)}, f32[14,64,256]{2,1,0:T(8,128)}, ...), condition=%wide.region_3.4_spmd, body=%wide.region_0.3_spmd.sunk | while | flops 411058176 | bytes 19072724 | solution.py:46
  97.1 3.3 fusion.34
  111.1 3.3 fusion.34
  125.1 3.3 fusion.34
  139.1 3.3 fusion.34
  153.1 3.3 fusion.34
  167.1 3.3 fusion.34
  181.1 3.3 fusion.34
  185.7 2.7 fusion.35
  195.1 3.3 fusion.34
  209.0 3.3 fusion.34
  223.0 3.3 fusion.34
  237.0 3.3 fusion.34
  251.0 3.3 fusion.34
  255.6 2.7 fusion.35
  265.0 3.3 fusion.34
  279.0 3.3 fusion.34
  296.1 3.9 fusion.12
  300.0 4.9 reshape.59
  306.8 73.6 %all-reduce = (f32[]{:T(128)}, f32[]{:T(128)}) all-reduce(f32[]{:T(128)} %reduce_sum.36, f32[]{:T(128)} %convert_reduce_fusion), channel_id=1, replica_groups=mesh['grid'=8,'wide'=32] {'grid','wide'}, use_global_device_ids=true, to_apply=%region_7.8 | all-reduce | flops 2 | bytes 16 | tf_op jit(solution)/shard_map/psum | solution.py:61
  383.3 166.5 %reduce-scatter.3.cloned.1.call-done = f32[128,256]{1,0:T(8,128)} async-done(((f32[4096,256]{1,0:T(8,128)}), f32[128,256]{1,0:T(8,128)}) %reduce-scatter.3.cloned.1.call-update) | async-done | bytes 131088 | tf_op jit(solution)/shard_map/reduce_scatter | solution.py:50
  (179 shorter events, 132.0 us)
Async XLA Ops:
  7.2 2.2 copy-start
  7.2 18.3 %copy-start.5 = (s32[14]{0:T(128)S(1)}, s32[14]{0:T(128)}, u32[]{:S(2)}) copy-start(s32[14]{0:T(128)} %param.11) | copy-start | bytes 172
  7.2 84.3 %all-gather.2.cloned.1.call-start = ((), (), s32[]{:S(2)}) async-start(), calls=%async_computation.2 | async-start | bytes 2162688 | tf_op jit(solution)/shard_map/all_gather | solution.py:43
  7.9 373.8 %reduce-scatter.5.cloned.1.call-start = ((), (), s32[]{:S(2)}) async-start(), calls=%async_computation.4 | async-start | bytes 1179648 | tf_op jit(solution)/shard_map/reduce_scatter | solution.py:58
  97.1 3.3 copy-start.1
  111.1 3.3 copy-start.1
  125.1 3.3 copy-start.1
  139.1 3.3 copy-start.1
  153.1 3.3 copy-start.1
  167.1 3.3 copy-start.1
  181.1 3.3 copy-start.1
  195.0 3.3 copy-start.1
  209.0 3.3 copy-start.1
  223.0 3.3 copy-start.1
  237.0 3.3 copy-start.1
  251.0 3.3 copy-start.1
  265.0 3.3 copy-start.1
  279.0 3.3 copy-start.1
  290.3 1.9 copy-start.4
  294.2 255.6 %reduce-scatter.3.cloned.1.call-start = ((), (), s32[]{:S(2)}) async-start(), calls=%async_computation.3 | async-start | bytes 4325376 | tf_op jit(solution)/shard_map/reduce_scatter | solution.py:50
  304.9 0.7 copy-start.6
  304.9 76.8 %copy-start.2 = (bf16[128,256]{1,0:T(8,128)(2,1)S(1)}, bf16[128,256]{1,0:T(8,128)(2,1)}, u32[]{:S(2)}) copy-start(bf16[128,256]{1,0:T(8,128)(2,1)} %param.16) | copy-start | bytes 196612
  304.9 244.9 %copy-start.3 = (bf16[128,256]{1,0:T(8,128)(2,1)S(1)}, bf16[128,256]{1,0:T(8,128)(2,1)}, u32[]{:S(2)}) copy-start(bf16[128,256]{1,0:T(8,128)(2,1)} %param.15) | copy-start | bytes 196612
Sparse Core Ops, SparseCore 0:
  10.6 80.8 all-gather.1
  294.3 28.5 reduce-scatter.4
  326.8 222.9 reduce-scatter.2
where the time goes:
time: 562 us; the launch traced here: 559 us
  waiting for transfers between devices  233 us (41%)
  matrix products  115 us (20%)
  blocking collectives  87.2 us (16%)
  local copies, waits for them, and re-layouts  52.6 us (9%)
  loops' own time  27.7 us (5%)
  other arithmetic  26.8 us (5%)
  between operations  16.3 us (3%)
    reduce_scatter x1, waiting for transfers between devices, per_device(): lax.psum_scatter(panel_grad.reshape(panel_blocks * side, width), 'wide',...  166 us
    psum x1, blocking collectives, per_device(): lax.psum((jnp.sum(loss_parts), jnp.sum(flags)), ('grid', 'wide'))  73.6 us
    all_gather x1, waiting for transfers between devices, per_device(): a_panel = lax.all_gather(factor_a, 'wide', axis=0, tiled=True)  66 us
    dot_general x14, matrix products, block_terms(): lax.dot_general(a_rows, khatri, (((1,), (1,)), ((), ())), preferred_eleme...  46.2 us
    dot_general x14, matrix products, block_terms(): grad_rows = jnp.dot(resid, khatri, preferred_element_type=jnp.float32)  37.5 us
    another operation x1, loops' own time, per_device(): lax.map(block_terms, (values, a_rows, b_rows, c_rows, flags))  27.7 us
    dot_general x14, matrix products, block_terms(): lax.dot_general(resid, a_rows, (((0,), (0,)), ((), ())), preferred_elemen...  26.9 us
    dot_general x14, local copies, waits for them, and re-layouts, block_terms(): lax.dot_general(resid, a_rows, (((0,), (0,)), ((), ())), preferred_elemen...  18.7 us
  transfers between devices with their start and end apart: 3, of which 2 were waited for; matrix products, arithmetic and copies ran while one was open for 3% of the time, Pallas kernels for 0%

commit v1 on v0

--- a/solution.py
+++ b/solution.py
@@ -40,7 +40,9 @@
     b_panel = lax.all_gather(factor_b, "grid", axis=0, tiled=True)
     b_rows = b_panel.reshape(-1, side, width)[b_block]
     c_rows = factor_c.reshape(-1, side, width)[c_block]
-    a_panel = lax.all_gather(factor_a, "wide", axis=0, tiled=True)
+    a_panel = jnp.concatenate(
+        lax.all_to_all(jnp.stack([factor_a] * lax.axis_size("wide")), "wide", 0, 0), axis=0
+    )
     a_rows = a_panel.reshape(-1, side, width)[a_block]
     flags = held.astype(jnp.float32)
     grad_rows, grad_cols, loss_parts = lax.map(block_terms, (values, a_rows, b_rows, c_rows, flags))

time: 562 us -> 543 us (0.966)
  waiting for transfers between devices: 233 us -> 201 us
  starting transfers between devices: 0.12 us -> 11.7 us
    all_gather x1 -> x0, waiting for transfers between devices: 66 us -> none  [per_device(): a_panel = lax.all_gather(factor_a, 'wide', axis=0, tiled=True)]
    all_to_all x0 -> x1, waiting for transfers between devices: none -> 34.7 us  [per_device(): lax.all_to_all(jnp.stack([factor_a] * lax.axis_size('wide')), 'wide', 0, 0)]
    all_to_all x0 -> x1, starting transfers between devices: none -> 11.6 us  [per_device(): lax.all_to_all(jnp.stack([factor_a] * lax.axis_size('wide')), 'wide', 0, 0)]
where the time goes in v1:
time: 543 us; the launch traced here: 540 us
  waiting for transfers between devices  201 us (37%)
  matrix products  115 us (21%)
  blocking collectives  88.2 us (16%)
  local copies, waits for them, and re-layouts  54.4 us (10%)
  loops' own time  27.7 us (5%)
  other arithmetic  24.8 us (5%)
  between operations  16.7 us (3%)
  starting transfers between devices  11.7 us (2%)
    reduce_scatter x1, waiting for transfers between devices, per_device(): lax.psum_scatter(panel_grad.reshape(panel_blocks * side, width), 'wide',...  166 us
    psum x1, blocking collectives, per_device(): lax.psum((jnp.sum(loss_parts), jnp.sum(flags)), ('grid', 'wide'))  74.9 us
    dot_general x14, matrix products, block_terms(): lax.dot_general(a_rows, khatri, (((1,), (1,)), ((), ())), preferred_eleme...  46.2 us
    dot_general x14, matrix products, block_terms(): grad_rows = jnp.dot(resid, khatri, preferred_element_type=jnp.float32)  37.5 us
    all_to_all x1, waiting for transfers between devices, per_device(): lax.all_to_all(jnp.stack([factor_a] * lax.axis_size('wide')), 'wide', 0, 0)  34.7 us
    another operation x1, loops' own time, per_device(): lax.map(block_terms, (values, a_rows, b_rows, c_rows, flags))  27.7 us
    dot_general x14, matrix products, block_terms(): lax.dot_general(resid, a_rows, (((0,), (0,)), ((), ())), preferred_elemen...  26.9 us
    dot_general x14, local copies, waits for them, and re-layouts, block_terms(): lax.dot_general(resid, a_rows, (((0,), (0,)), ((), ())), preferred_elemen...  18.7 us
  transfers between devices with their start and end apart: 3, of which 2 were waited for; matrix products, arithmetic and copies ran while one was open for 3% of the time, Pallas kernels for 0%

profile of v1, /device:TPU:8, one launch (start us, length us, event | category | flops | bytes accessed | tf_op | source)
XLA Modules:
  0.0 539.9 jit_solution(7554224967395443461)
XLA Ops:
  9.7 11.6 %all-to-all-start = ((bf16[32,128,256]{2,1,0:T(8,128)(2,1)}), bf16[32,128,256]{2,1,0:T(8,128)(2,1)}, u32[]{:S(2)}, u32[]{:S(2)}) async-start(bf16[32,128,256]{2,1,0:T(8,128)(2,1)} %stack.2), calls=%async_computation | async-start | bytes 4194304 | tf_op jit(solution)/shard_map/all_to_all | solution.py:44
  22.1 13.3 %all_gather.3 = bf16[1024,256]{1,0:T(8,128)(2,1)S(1)} all-gather(bf16[128,256]{1,0:T(8,128)(2,1)S(1)} %copy-done.2), channel_id=1, replica_groups=mesh['grid'=8,'wide'=32] {'grid'}, dimensions={0}, use_global_device_ids=true | all-gather | bytes 589824 | tf_op jit(solution)/shard_map/all_gather | solution.py:40
  36.8 34.7 %all-to-all-done = bf16[32,128,256]{2,1,0:T(8,128)(2,1)} async-done(((bf16[32,128,256]{2,1,0:T(8,128)(2,1)}), bf16[32,128,256]{2,1,0:T(8,128)(2,1)}, u32[]{:S(2)}, u32[]{:S(2)}) %all-to-all-start) | async-done | bytes 2097184 | tf_op jit(solution)/shard_map/all_to_all | solution.py:44
  71.4 2.9 gather_fusion
  74.4 195.8 %while.14 = (s32[]{:T(128)}, f32[14,64,256]{2,1,0:T(8,128)}, f32[14,64,256]{2,1,0:T(8,128)}, f32[14]{0:T(128)S(1)}, bf16[14,64,256]{2,1,0:T(8,128)(2,1)}, /*inde...) while((s32[]{:T(128)}, f32[14,64,256]{2,1,0:T(8,128)}, ...), condition=%wide.region_3.4_spmd, body=%wide.region_0.3_spmd.sunk | while | flops 411058176 | bytes 19072724 | solution.py:48
  77.1 3.3 fusion.34
  81.7 2.7 fusion.35
  91.1 3.3 fusion.34
  105.1 3.3 fusion.34
  119.1 3.3 fusion.34
  133.1 3.3 fusion.34
  147.0 3.3 fusion.34
  161.0 3.3 fusion.34
  175.0 3.3 fusion.34
  189.0 3.3 fusion.34
  203.0 3.3 fusion.34
  217.0 3.3 fusion.34
  231.0 3.3 fusion.34
  245.0 3.3 fusion.34
  258.9 3.3 fusion.34
  276.0 3.9 fusion.12
  279.9 4.9 reshape.57
  286.1 74.9 %all-reduce = (f32[]{:T(128)}, f32[]{:T(128)}) all-reduce(f32[]{:T(128)} %reduce_sum.36, f32[]{:T(128)} %convert_reduce_fusion), channel_id=1, replica_groups=mesh['grid'=8,'wide'=32] {'grid','wide'}, use_global_device_ids=true, to_apply=%region_7.8 | all-reduce | flops 2 | bytes 16 | tf_op jit(solution)/shard_map/psum | solution.py:63
  363.9 166.5 %reduce-scatter.3.cloned.1.call-done = f32[128,256]{1,0:T(8,128)} async-done(((f32[4096,256]{1,0:T(8,128)}), f32[128,256]{1,0:T(8,128)}) %reduce-scatter.3.cloned.1.call-update) | async-done | bytes 131088 | tf_op jit(solution)/shard_map/reduce_scatter | solution.py:52
  (181 shorter events, 133.9 us)
Async XLA Ops:
  7.2 14.3 %copy-start = (bf16[4096,256]{1,0:T(8,128)(2,1)S(1)}, bf16[4096,256]{1,0:T(8,128)(2,1)}, u32[]{:S(2)}) copy-start(bf16[4096,256]{1,0:T(8,128)(2,1)} %param.17) | copy-start | bytes 6291460
  9.7 11.7 %copy-start.7 = (s32[14]{0:T(128)S(1)}, s32[14]{0:T(128)}, u32[]{:S(2)}) copy-start(s32[14]{0:T(128)} %param.14) | copy-start | bytes 172
  9.7 11.7 %copy-start.6 = (s32[14]{0:T(128)S(1)}, s32[14]{0:T(128)}, u32[]{:S(2)}) copy-start(s32[14]{0:T(128)} %param.13) | copy-start | bytes 172
  9.7 12.3 %copy-start.4 = (s32[14]{0:T(128)S(1)}, s32[14]{0:T(128)}, u32[]{:S(2)}) copy-start(s32[14]{0:T(128)} %param.12) | copy-start | bytes 172
  9.7 12.4 %copy-start.2 = (bf16[128,256]{1,0:T(8,128)(2,1)S(1)}, bf16[128,256]{1,0:T(8,128)(2,1)}, u32[]{:S(2)}) copy-start(bf16[128,256]{1,0:T(8,128)(2,1)} %param.16) | copy-start | bytes 196612
  9.7 61.7 %all-to-all-start = ((bf16[32,128,256]{2,1,0:T(8,128)(2,1)}), bf16[32,128,256]{2,1,0:T(8,128)(2,1)}, u32[]{:S(2)}, u32[]{:S(2)}) async-start(bf16[32,128,256]{2,1,0:T(8,128)(2,1)} %stack.2), calls=%async_computation | async-start | bytes 4194304 | tf_op jit(solution)/shard_map/all_to_all | solution.py:44
  21.3 15.5 %copy-start.5 = (s32[14]{0:T(128)S(1)}, s32[14]{0:T(128)}, u32[]{:S(2)}) copy-start(s32[14]{0:T(128)} %param.11) | copy-start | bytes 172
  21.3 341.0 %reduce-scatter.5.cloned.1.call-start = ((), (), s32[]{:S(2)}) async-start(), calls=%async_computation.4 | async-start | bytes 1179648 | tf_op jit(solution)/shard_map/reduce_scatter | solution.py:60
  77.1 3.3 copy-start.1
  91.1 3.3 copy-start.1
  105.1 3.3 copy-start.1
  119.1 3.3 copy-start.1
  133.1 3.3 copy-start.1
  147.0 3.3 copy-start.1
  161.0 3.3 copy-start.1
  175.0 3.3 copy-start.1
  189.0 3.3 copy-start.1
  203.0 3.3 copy-start.1
  217.0 3.3 copy-start.1
  231.0 3.3 copy-start.1
  245.0 3.3 copy-start.1
  258.9 3.3 copy-start.1
  274.1 256.3 %reduce-scatter.3.cloned.1.call-start = ((), (), s32[]{:S(2)}) async-start(), calls=%async_computation.3 | async-start | bytes 4325376 | tf_op jit(solution)/shard_map/reduce_scatter | solution.py:52
  284.8 245.5 %copy-start.3 = (bf16[128,256]{1,0:T(8,128)(2,1)S(1)}, bf16[128,256]{1,0:T(8,128)(2,1)}, u32[]{:S(2)}) copy-start(bf16[128,256]{1,0:T(8,128)(2,1)} %param.15) | copy-start | bytes 196612
Sparse Core Ops, SparseCore 0:
  274.2 28.8 reduce-scatter.4
  307.0 223.3 reduce-scatter.2
